TPU v7x, 1024 devices: a whole 4x8x16 slice. The times are simulated.
1024 devices in a mesh: dp: 32 (over z_lo, y), tensor: 32 (over z_hi, x, core).
Axes of the slice: x: 4, y: 8, z: 16 (z_hi: 4, z_lo: 4; z = z_hi * 4 + z_lo), core: 2. Of those that a mesh axis runs over, the one named last changes fastest.
Arguments:
- local_gate: bfloat16 [14336, 16384], P('tensor', 'dp'), may hold values from -6 to 6
- local_up: bfloat16 [14336, 16384], P('tensor', 'dp'), may hold values from -6 to 6
- local_grad: bfloat16 [16384, 4096], P('dp'), may hold values from -48 to 48
- orphan_gate: bfloat16 [14336, 1024], P('tensor', 'dp'), may hold values from -6 to 6
- orphan_up: bfloat16 [14336, 1024], P('tensor', 'dp'), may hold values from -6 to 6
- orphan_grad: bfloat16 [1024, 4096], P('dp'), may hold values from -48 to 48
- orphan_len: int32 [32], P('dp'), may hold values from 1 to 32, 896 in all
- orphan_dest: int32 [1024, 1], P('dp'), may hold values from 0 to 31; in each aligned block of 32 rows (0 to 31, 32 to 63, ...) at most 2 rows name the same one
- loop_order: int32 [32], replicated, may hold values from 0 to 31, each once
Outputs:
- down_grad: float32 [14336, 4096], P('tensor', 'dp')
- orphan_load: float32 [32], P('dp')
Inputs may be any that keep to these rules, and one draw needn't show every extreme that they name: `orphan_dest`: among the 32 rows of one holder, at most 2 name the same replica, live or not, and some holder's rows reach 2 for some replica. `loop_order`: A permutation of the replicas.
All inputs are finite; a program needn't handle non-finite values. No bound on the sum of `orphan_len` on one device may be relied on, other than what follows from the above.
Results may differ from a plain program's by a relative error of at most 0.0041.
Values may be sent and summed in bfloat16 or wider, within the bound.
No kernel may reach another device: no remote copies, remote signals or barrier semaphores. Data moves between devices by JAX's collectives and lax.ppermute only.
A program may use at most 32 MiB of HBM per device.

v0:
```python
import jax
import jax.numpy as jnp
from jax import lax
from jax.sharding import Mesh
from jax.sharding import PartitionSpec as P

DP = ("dp_0", "dp_1")


def copy_for_each(array, axis):
    copies = jnp.broadcast_to(array, (lax.axis_size(axis), *array.shape))
    return lax.all_to_all(copies, axis, split_axis=0, concat_axis=0, tiled=True)


def over_copies(array, axis):
    return copy_for_each(array, axis).sum(axis=0)


def own_block(pieces, axes, sequence):
    inside = pieces.shape[1:]
    pieces = pieces.reshape(*(lax.axis_size(a) for a in axes), *inside)
    pieces = jnp.moveaxis(pieces, sequence, range(len(axes))).reshape(-1, *inside)
    for k in sequence:
        pieces = lax.psum_scatter(pieces, axes[k], scatter_dimension=0, tiled=True)
    return pieces[0]


def in_blocks(array, dim, length):
    before, after = (array.shape[:dim], array.shape[dim + 1 :])
    return jnp.moveaxis(array.reshape(*before, length, -1, *after), dim, 0)


def scatter_axes(array, axes, sequence, dim):
    length = lax.axis_size(axes)
    return own_block(in_blocks(array, dim, length), axes, sequence)


def hidden_of(gate, upper):
    return (jax.nn.silu(gate.astype(jnp.float32)) * upper.astype(jnp.float32)).astype(jnp.bfloat16)


def scaled_rows(grads, factors):
    return (grads.astype(jnp.float32) * factors[:, None]).astype(jnp.bfloat16)


def per_device(
    local_gate,
    local_up,
    local_grad,
    orphan_gate,
    orphan_up,
    orphan_grad,
    orphan_len,
    orphan_dest,
    loop_order,
):
    replicas = lax.axis_size(DP)
    own_rows = local_grad.shape[0]
    orphan_count = orphan_grad.shape[0]
    width = local_grad.shape[1]
    block_cols = width // replicas
    targets = orphan_dest[:, 0]
    live_rows = (jnp.arange(orphan_count, dtype=jnp.int32) < orphan_len[0]).astype(jnp.float32)
    one_hot = (targets[:, None] == jnp.arange(replicas, dtype=jnp.int32)[None, :]).astype(
        jnp.float32
    )
    own_hidden = hidden_of(local_gate, local_up)
    orphan_hidden = hidden_of(orphan_gate, orphan_up)
    per_target = over_copies(jnp.sum(one_hot * live_rows[:, None], axis=0), DP)
    weights = 1.0 / (own_rows + per_target)
    received = lax.dynamic_slice_in_dim(per_target, lax.axis_index(DP), 1)
    own_weight = lax.dynamic_slice_in_dim(weights, lax.axis_index(DP), 1)
    extra_scaled = scaled_rows(orphan_grad, jnp.sum(one_hot * weights[None, :], axis=1) * live_rows)
    own_scaled = scaled_rows(local_grad, jnp.broadcast_to(own_weight, (own_rows,)))

    def reorder(scaled):
        row_total = scaled.shape[0]
        return jnp.take(
            scaled.reshape(row_total, replicas, block_cols), loop_order, axis=1
        ).reshape(row_total, width)

    terms = jnp.dot(own_hidden, reorder(own_scaled), preferred_element_type=jnp.float32)
    terms = terms + jnp.dot(
        orphan_hidden, reorder(extra_scaled), preferred_element_type=jnp.float32
    )
    grad_share = scatter_axes(terms, DP, (1, 0), 1)
    return (grad_share, received / orphan_count)


def solution(mesh):
    torus = Mesh(mesh.devices.reshape(4, 8, mesh.shape["tensor"]), ("dp_0", "dp_1", "tensor"))
    return jax.shard_map(
        per_device,
        mesh=torus,
        in_specs=(
            P("tensor", DP),
            P("tensor", DP),
            P(DP, None),
            P("tensor", DP),
            P("tensor", DP),
            P(DP, None),
            P(DP),
            P(DP, None),
            P(),
        ),
        out_specs=(P("tensor", DP), P(DP)),
        check_vma=False,
    )
```

profile of v0, /device:TPU:1, one launch (start us, length us, event | category | flops | bytes accessed | tf_op | source)
XLA Modules:
  0.0 218.5 jit_solution(10033427308022054592)
XLA Ops:
  7.8 0.7 select_reduce_fusion.1
  8.6 0.6 broadcast_in_dim.36
  9.2 13.5 %all-to-all-start = ((f32[32,1,32]{2,1,0:T(1,128)}), f32[32,1,32]{2,1,0:T(1,128)S(1)}, u32[]{:S(2)}, u32[]{:S(2)}) async-start(f32[32,1,32]{2,1,0:T(1,128)} %broadcast_in_dim.36), calls=%async_computation | async-start | bytes 32768 | tf_op jit(solution)/shard_map/all_to_all | solution.py:12
  22.6 0.0 reduce-scatter.3.cloned.1.call-start
  22.7 0.7 compare_and_fusion
  23.4 0.7 compare_select_fusion
  24.0 0.1 broadcast_bitcast_fusion
  24.1 0.0 copy-start.5
  24.1 6.6 %copy.25 = bf16[512,4096]{0,1:T(8,128)(2,1)} copy(bf16[512,4096]{1,0:T(8,128)(2,1)} %param.11) | data formatting | bytes 8388608 | tf_op args[2]
  30.7 0.9 all-to-all-done
  31.6 0.0 copy-done.5
  31.6 0.2 select_reduce_fusion
  31.8 0.6 dynamic_slice.8
  32.4 5.6 %multiply_convert_fusion = bf16[512,4096]{0,1:T(8,128)(2,1)} fusion(bf16[512,4096]{0,1:T(8,128)(2,1)} %copy.25, f32[]{:T(128)} %bitcast.4), kind=kLoop, calls=%fused_computation.2 | loop fusion | flops 6291456 | bytes 8388612 | tf_op jit(solution)/shard_map/convert_element_type | solution.py:43
  38.0 0.0 copy-start.2
  38.0 6.5 %copy.27 = bf16[512,32,128]{2,0,1:T(8,128)(2,1)} copy(bf16[512,32,128]{0,2,1:T(8,128)(2,1)} %bitcast.39) | data formatting | bytes 8388608 | tf_op jit(solution)/shard_map/reshape | solution.py:79
  44.5 0.0 copy-done.2
  44.5 0.1 copy_bitcast_fusion
  44.6 0.6 gather_fusion.1
  45.2 5.2 %gather_fusion = bf16[32,512,128]{2,1,0:T(8,128)(2,1)} fusion(bf16[512,32,128]{2,0,1:T(8,128)(2,1)} %copy.27, s32[1024]{0:T(1024)S(1)} %pad_clamp_fusion), kind=kCustom, calls=%fused_computation | custom fusion | bytes 8388736 | tf_op jit(solution)/shard_map/jit(_take)/gather | solution.py:78
  50.4 6.5 %copy.28 = bf16[512,32,128]{0,2,1:T(8,128)(2,1)} copy(bf16[512,32,128]{2,0,1:T(8,128)(2,1)} %bitcast.40) | data formatting | bytes 8388608 | tf_op jit(solution)/shard_map/jit(_take)/gather | solution.py:78
  56.9 0.0 copy-start
  56.9 0.0 copy-start.1
  56.9 2.7 %bitcast_select_fusion = bf16[512,4096]{0,1:T(8,128)(2,1)S(1)} fusion(bf16[512,32,128]{0,2,1:T(8,128)(2,1)} %copy.28, pred[4096]{0:T(1024)(128)(4,1)S(1)} %broadcast_bitcast_fusion), kind=kLoop, calls=%fused_computation.4 | loop fusion | flops 2097152 | bytes 8392704 | tf_op jit(solution)/shard_map/jit(_take)/select_n | solution.py:78
  59.6 0.0 copy-done
  59.6 0.0 copy-done.1
  59.6 0.0 copy-start.3
  59.6 0.0 copy-start.4
  59.6 2.1 fusion.5
  61.8 0.0 copy-done.3
  61.8 0.0 copy-done.4
  61.8 1.2 add_bitcast_fusion
  63.0 1.6 copy.34
  64.5 7.2 %copy.31 = f32[4,8,448,128]{3,2,0,1:T(8,128)} copy(f32[4,8,448,128]{3,1,0,2:T(8,128)S(1)} %bitcast.38) | data formatting | bytes 14680064 | tf_op jit(solution)/shard_map/reshape | solution.py:21
  71.8 0.0 reduce-scatter.3.cloned.1.call-update
  71.8 0.0 reduce-scatter.5.cloned.1.call-start
  71.8 97.1 %reduce-scatter.3.cloned.1.call-done = f32[4,448,128]{2,1,0:T(8,128)} async-done(((f32[32,448,128]{2,1,0:T(8,128)}), f32[4,448,128]{2,1,0:T(8,128)}) %reduce-scatter.3.cloned.1.call-update) | async-done | bytes 917520 | tf_op jit(solution)/shard_map/reduce_scatter | solution.py:24
  168.9 0.0 reduce-scatter.5.cloned.1.call-update
  168.9 0.6 dynamic_slice.10
  170.2 40.4 %reduce-scatter.5.cloned.1.call-done = f32[1,448,128]{2,1,0:T(8,128)} async-done(((f32[4,448,128]{2,1,0:T(8,128)}), f32[1,448,128]{2,1,0:T(8,128)}) %reduce-scatter.5.cloned.1.call-update) | async-done | bytes 229392 | tf_op jit(solution)/shard_map/reduce_scatter | solution.py:24
  (5 shorter events, 0.0 us)
Async XLA Ops:
  9.2 22.4 %all-to-all-start = ((f32[32,1,32]{2,1,0:T(1,128)}), f32[32,1,32]{2,1,0:T(1,128)S(1)}, u32[]{:S(2)}, u32[]{:S(2)}) async-start(f32[32,1,32]{2,1,0:T(1,128)} %broadcast_in_dim.36), calls=%async_computation | async-start | bytes 32768 | tf_op jit(solution)/shard_map/all_to_all | solution.py:12
  22.6 146.2 %reduce-scatter.3.cloned.1.call-start = ((), (), s32[]{:S(2)}) async-start(), calls=%async_computation.3 | async-start | bytes 8257536 | tf_op jit(solution)/shard_map/reduce_scatter | solution.py:24
  24.1 7.5 %copy-start.5 = (s32[32,1]{0,1:T(1,128)S(1)}, s32[32,1]{0,1:T(1,128)}, u32[]{:S(2)}) copy-start(s32[32,1]{0,1:T(1,128)} %param.16) | copy-start | bytes 388
  38.0 6.5 %copy-start.2 = (bf16[32,4096]{1,0:T(8,128)(2,1)S(1)}, bf16[32,4096]{1,0:T(8,128)(2,1)}, u32[]{:S(2)}) copy-start(bf16[32,4096]{1,0:T(8,128)(2,1)} %param.14) | copy-start | bytes 786436
  56.9 2.7 %copy-start = (bf16[448,512]{1,0:T(8,128)(2,1)S(1)}, bf16[448,512]{1,0:T(8,128)(2,1)}, u32[]{:S(2)}) copy-start(bf16[448,512]{1,0:T(8,128)(2,1)} %param.10) | copy-start | bytes 1376260
  56.9 2.7 %copy-start.1 = (bf16[448,512]{1,0:T(8,128)(2,1)S(1)}, bf16[448,512]{1,0:T(8,128)(2,1)}, u32[]{:S(2)}) copy-start(bf16[448,512]{1,0:T(8,128)(2,1)} %param.9) | copy-start | bytes 1376260
  59.6 2.2 copy-start.3
  59.6 2.2 copy-start.4
  71.8 138.7 %reduce-scatter.5.cloned.1.call-start = ((), (), s32[]{:S(2)}) async-start(), calls=%async_computation.4 | async-start | bytes 1146880 | tf_op jit(solution)/shard_map/reduce_scatter | solution.py:24
Sparse Core Ops, SparseCore 0:
  71.9 96.9 reduce-scatter.2
  172.9 37.5 reduce-scatter.4
where the time goes:
time: 219 us; the launch traced here: 218 us
  waiting for transfers between devices  138 us (63%)
  local copies, waits for them, and re-layouts  36 us (16%)
  between operations  16.6 us (8%)
  starting transfers between devices  13.5 us (6%)
  other arithmetic  10.7 us (5%)
  matrix products  3.3 us (2%)
    reduce_scatter x2, waiting for transfers between devices, own_block(): pieces = lax.psum_scatter(pieces, axes[k], scatter_dimension=0, tiled=True)  137 us
    all_to_all x1, starting transfers between devices, copy_for_each(): return lax.all_to_all(copies, axis, split_axis=0, concat_axis=0, tiled=True)  13.5 us
    gather x3, local copies, waits for them, and re-layouts, reorder(): jnp.take(scaled.reshape(row_total, replicas, block_cols), loop_order, axi...  12.3 us
    unnamed x14, local copies, waits for them, and re-layouts  8.14 us
    reshape x1, local copies, waits for them, and re-layouts, own_block(): pieces = pieces.reshape(*(lax.axis_size(a) for a in axes), *inside)  7.22 us
    reshape x1, local copies, waits for them, and re-layouts, reorder(): scaled.reshape(row_total, replicas, block_cols)  6.45 us
    convert_element_type x1, other arithmetic, scaled_rows(): return (grads.astype(jnp.float32) * factors[:, None]).astype(jnp.bfloat16)  5.63 us
  transfers between devices with their start and end apart: 3, of which 3 were waited for; matrix products, arithmetic and copies ran while one was open for 4% of the time, Pallas kernels for 0%

commit v1 on v0

v1 whole, which is shorter than its diff:
```python
import jax
import jax.numpy as jnp
from jax import lax
from jax.experimental import pallas as pl
from jax.experimental.pallas import tpu as pltpu
from jax.sharding import Mesh
from jax.sharding import PartitionSpec as P

DP = ("dp_0", "dp_1")


def hidden_of(gate, upper):
    gate = gate.astype(jnp.float32)
    return gate / (1.0 + jnp.exp(-gate)) * upper.astype(jnp.float32)


def partial_kernel(
    order_ref,
    place_ref,
    len_ref,
    counts_ref,
    dest_ref,
    gate_ref,
    up_ref,
    orphan_gate_ref,
    orphan_up_ref,
    grad_ref,
    orphan_grad_ref,
    out_ref,
    hidden_ref,
):
    own_rows, _ = grad_ref.shape
    orphans = orphan_grad_ref.shape[0]
    replicas, _, cols = out_ref.shape
    hidden_ref[:, :own_rows] = hidden_of(gate_ref[...], up_ref[...]).astype(jnp.bfloat16)
    extra = hidden_of(orphan_gate_ref[...], orphan_up_ref[...])
    hidden_ref[:, own_rows:] = extra.T.astype(jnp.bfloat16)

    weights = 1.0 / (own_rows + jnp.sum(counts_ref[...], axis=0, keepdims=True))
    lanes = lax.broadcasted_iota(jnp.int32, (1, replicas), 1)
    own_weight = jnp.sum(jnp.where(lanes == place_ref[0], weights, 0.0), axis=1, keepdims=True)
    one_hot = (dest_ref[...] == lax.broadcasted_iota(jnp.int32, (orphans, replicas), 1)).astype(
        jnp.float32
    )
    live = (lax.broadcasted_iota(jnp.int32, (orphans, 1), 0) < len_ref[0]).astype(jnp.float32)
    factors = jnp.sum(one_hot * weights, axis=1, keepdims=True) * live

    def scaled_block(slot):
        at = pl.ds(pl.multiple_of(order_ref[slot] * cols, cols), cols)
        own = grad_ref[:, at].astype(jnp.float32) * own_weight
        extra = orphan_grad_ref[:, at].astype(jnp.float32) * factors
        return jnp.concatenate([own.astype(jnp.bfloat16), extra.astype(jnp.bfloat16)], axis=0)

    def step(pair, carry):
        left, right = 2 * pair, 2 * pair + 1
        both = jnp.concatenate([scaled_block(left), scaled_block(right)], axis=1)
        term = jnp.dot(hidden_ref[...], both, preferred_element_type=jnp.float32)
        out_ref[left] = term[:, :cols].astype(jnp.bfloat16)
        out_ref[right] = term[:, cols:].astype(jnp.bfloat16)
        return carry

    lax.fori_loop(0, replicas // 2, step, 0, unroll=2)


def partial_blocks(order, place, length, counts, dest, gate, up, o_gate, o_up, grad, o_grad):
    replicas = order.shape[0]
    rows, own_rows = gate.shape
    cols = grad.shape[1] // replicas
    orphans = o_grad.shape[0]
    smem = pl.BlockSpec(memory_space=pltpu.SMEM)
    vmem = pl.BlockSpec(memory_space=pltpu.VMEM)
    depth = own_rows + orphans
    return pl.pallas_call(
        partial_kernel,
        out_shape=jax.ShapeDtypeStruct((replicas, rows, cols), jnp.bfloat16),
        in_specs=[smem] * 3 + [vmem] * 8,
        out_specs=vmem,
        scratch_shapes=[pltpu.VMEM((rows, depth), jnp.bfloat16)],
        cost_estimate=pl.CostEstimate(
            flops=2 * rows * depth * grad.shape[1],
            bytes_accessed=2 * depth * grad.shape[1] + 2 * rows * grad.shape[1],
            transcendentals=rows * depth,
        ),
    )(order, place, length, counts, dest, gate, up, o_gate, o_up, grad, o_grad)


def per_device(
    local_gate,
    local_up,
    local_grad,
    orphan_gate,
    orphan_up,
    orphan_grad,
    orphan_len,
    orphan_dest,
    loop_order,
):
    replicas = lax.axis_size(DP)
    place = lax.axis_index(DP)
    orphans = orphan_grad.shape[0]
    live = jnp.arange(orphans, dtype=jnp.int32) < orphan_len[0]
    hits = (orphan_dest == jnp.arange(replicas, dtype=jnp.int32)[None, :]) & live[:, None]
    mine = jnp.sum(hits.astype(jnp.float32), axis=0)
    counts = jnp.broadcast_to(mine[None, None], (replicas, 1, replicas))
    counts = lax.all_to_all(counts, DP, split_axis=0, concat_axis=0, tiled=True)
    counts = counts.reshape(replicas, replicas)
    load = lax.dynamic_slice_in_dim(jnp.sum(counts, axis=0), place, 1) / orphans
    blocks = partial_blocks(
        loop_order,
        place.astype(jnp.int32).reshape(1),
        orphan_len,
        counts,
        orphan_dest,
        local_gate,
        local_up,
        orphan_gate.T,
        orphan_up.T,
        local_grad,
        orphan_grad,
    )
    blocks = lax.all_to_all(blocks, DP, split_axis=0, concat_axis=0, tiled=True)
    return jnp.sum(blocks.astype(jnp.float32), axis=0), load


def solution(mesh):
    torus = Mesh(mesh.devices.reshape(4, 8, mesh.shape["tensor"]), ("dp_0", "dp_1", "tensor"))
    return jax.shard_map(
        per_device,
        mesh=torus,
        in_specs=(
            P("tensor", DP),
            P("tensor", DP),
            P(DP, None),
            P("tensor", DP),
            P("tensor", DP),
            P(DP, None),
            P(DP),
            P(DP, None),
            P(),
        ),
        out_specs=(P("tensor", DP), P(DP)),
        check_vma=False,
    )
```

time: 219 us -> 163 us (0.74)
  the two profiles are of different devices: /device:TPU:1 before, /device:TPU:590 now
where the time goes in v1:
time: 163 us
  waiting for transfers between devices  125 us (77%)
  starting transfers between devices  17.3 us (11%)
  Pallas kernels  9.9 us (6%)
  other arithmetic  4.06 us (2%)
  local copies, waits for them, and re-layouts  3.15 us (2%)
  between operations  3.1 us (2%)
    all_to_all x1, waiting for transfers between devices, per_device(): blocks = lax.all_to_all(blocks, DP, split_axis=0, concat_axis=0, tiled=True)  119 us
    all_to_all x1, starting transfers between devices, per_device(): counts = lax.all_to_all(counts, DP, split_axis=0, concat_axis=0, tiled=True)  10.4 us
    pallas_call x1, Pallas kernels, partial_blocks(): pl.pallas_call(partial_kernel, out_shape=jax.ShapeDtypeStruct((replicas,...  9.9 us
    all_to_all x1, starting transfers between devices, per_device(): blocks = lax.all_to_all(blocks, DP, split_axis=0, concat_axis=0, tiled=True)  6.9 us
    all_to_all x1, waiting for transfers between devices, per_device(): counts = lax.all_to_all(counts, DP, split_axis=0, concat_axis=0, tiled=True)  6.67 us
  transfers between devices with their start and end apart: 2, of which 2 were waited for; matrix products, arithmetic and copies ran while one was open for 1% of the time, Pallas kernels for 0%

profile of v1, /device:TPU:590, one launch (start us, length us, event | category | flops | bytes accessed | tf_op | source)
XLA Modules:
  0.0 162.8 jit_solution(3104841660633748698)
XLA Ops:
  1.3 0.7 convert_reduce_fusion.1
  2.0 0.6 broadcast_in_dim.2
  2.7 10.4 %all-to-all-start = ((f32[32,1,32]{2,1,0:T(1,128)}), f32[32,1,32]{2,1,0:T(1,128)S(1)}, u32[]{:S(2)}, u32[]{:S(2)}) async-start(f32[32,1,32]{2,1,0:T(1,128)} %broadcast_in_dim.2), calls=%async_computation | async-start | bytes 32768 | tf_op jit(solution)/shard_map/all_to_all | solution.py:105
  13.1 1.3 copy.13.dest_ref
  14.4 6.7 %all-to-all-done = f32[32,1,32]{2,1,0:T(1,128)S(1)} async-done(((f32[32,1,32]{2,1,0:T(1,128)}), f32[32,1,32]{2,1,0:T(1,128)S(1)}, u32[]{:S(2)}, u32[]{:S(2)}) %all-to-all-start) | async-done | bytes 4128 | tf_op jit(solution)/shard_map/all_to_all | solution.py:105
  21.1 0.0 copy-start
  21.1 0.6 copy-done
  21.7 9.9 %shard_map.104 = bf16[32,448,128]{2,1,0:T(8,128)(2,1)} custom-call(s32[32]{0:T(128)} %order_ref.1, s32[1]{0:T(128)} %bitcast.place_ref, s32[1]{0:T(128)} %copy.14.len_ref, f32[32,32]{1,0:T(8,128)} %bitcast.7, s32[32,1]{1,0:T(8,128)} %copy.13.dest_ref, bf16[448,512]{1,0:T(8,128)(2,1)} %gate_ref.1, bf16[448,512]{1,0:T(8,128)(2,1)} %up_ref.1, ...), custom_call_target="tpu_custom_call" | custom-call | flops 1996488704 | bytes 8126464 | tf_op jit(solution)/shard_map/pallas_call | solution.py:73
  31.6 0.0 copy-start.1
  31.6 6.9 %all-to-all-start.1 = ((bf16[32,448,128]{2,1,0:T(8,128)(2,1)}), bf16[32,448,128]{2,1,0:T(8,128)(2,1)}, u32[]{:S(2)}, u32[]{:S(2)}) async-start(bf16[32,448,128]{2,1,0:T(8,128)(2,1)} %shard_map.104), calls=%async_computation.1 | async-start | bytes 7340032 | tf_op jit(solution)/shard_map/all_to_all | solution.py:121
  38.5 0.0 copy-done.1
  38.5 0.1 reduce_sum.29
  38.6 0.6 dynamic_slice.3
  39.8 118.6 %all-to-all-done.1 = bf16[32,448,128]{2,1,0:T(8,128)(2,1)} async-done(((bf16[32,448,128]{2,1,0:T(8,128)(2,1)}), bf16[32,448,128]{2,1,0:T(8,128)(2,1)}, u32[]{:S(2)}, u32[]{:S(2)}) %all-to-all-start.1) | async-done | bytes 3670048 | tf_op jit(solution)/shard_map/all_to_all | solution.py:121
  158.4 3.3 %convert_reduce_fusion = f32[448,128]{1,0:T(8,128)} fusion(bf16[32,448,128]{2,1,0:T(8,128)(2,1)} %all-to-all-done.1), kind=kLoop, calls=%fused_computation | loop fusion | flops 3612672 | bytes 3899392 | tf_op jit(solution)/shard_map/reduce_sum | solution.py:122
  (1 shorter events, 0.0 us)
Async XLA Ops:
  2.7 18.4 %all-to-all-start = ((f32[32,1,32]{2,1,0:T(1,128)}), f32[32,1,32]{2,1,0:T(1,128)S(1)}, u32[]{:S(2)}, u32[]{:S(2)}) async-start(f32[32,1,32]{2,1,0:T(1,128)} %broadcast_in_dim.2), calls=%async_computation | async-start | bytes 32768 | tf_op jit(solution)/shard_map/all_to_all | solution.py:105
  21.1 0.6 copy-start
  31.6 6.9 %copy-start.1 = (f32[32,1,32]{2,1,0:T(1,128)S(1)}, f32[32,1,32]{2,1,0:T(1,128)}, u32[]{:S(2)}) copy-start(f32[32,1,32]{2,1,0:T(1,128)} %copy-done) | copy-start | bytes 12292
  31.6 126.8 %all-to-all-start.1 = ((bf16[32,448,128]{2,1,0:T(8,128)(2,1)}), bf16[32,448,128]{2,1,0:T(8,128)(2,1)}, u32[]{:S(2)}, u32[]{:S(2)}) async-start(bf16[32,448,128]{2,1,0:T(8,128)(2,1)} %shard_map.104), calls=%async_computation.1 | async-start | bytes 7340032 | tf_op jit(solution)/shard_map/all_to_all | solution.py:121
